TPU v7x, 128 devices: a whole 4x4x4 slice. The times are simulated.
128 devices in a mesh: tm: 16 (over z_hi, y, core), space: 8 (over x, z_lo).
Axes of the slice: x: 4, y: 4, z: 4 (z_hi: 2, z_lo: 2; z = z_hi * 2 + z_lo), core: 2. Of those that a mesh axis runs over, the one named last changes fastest.
Arguments:
- tokens: bfloat16 [64, 24, 80, 1024], P('tm', 'space'), may hold values from -6 to 6
- w_in: bfloat16 [1024, 4416], replicated, may hold values from -0.1875 to 0.1875
- w_out: bfloat16 [2048, 1024], replicated, may hold values from -0.125 to 0.125
- a_log_time: float32 [32], replicated, may hold values from -16 to -3
- a_log_space: float32 [32], replicated, may hold values from -14 to -3
- dt_bias_time: float32 [32], replicated, may hold values from -1 to 1
- dt_bias_space: float32 [32], replicated, may hold values from -1 to 1
- skip_time: float32 [32], replicated, may hold values from 0.5 to 1.5
- skip_space: float32 [32], replicated, may hold values from 0.5 to 1.5
- norm_gain: float32 [2048], replicated, may hold values from 0.25 to 1.75
Outputs:
- mixed: bfloat16 [64, 24, 80, 1024], P('tm', 'space')
All inputs are finite; a program needn't handle non-finite values.
Results may differ from a plain program's by a relative error of at most 0.0062.
The roundings to bfloat16 on the way count: a program that leaves them out, or rounds other values in their place, can miss the bound.
Values may be sent and summed in bfloat16 or wider, within the bound.
A program may use at most 192 MiB of HBM per device.

v0:
```python
import jax
import jax.numpy as jnp
from jax import lax
from jax.sharding import PartitionSpec as P

D = 1024
HEADS = 32
HEAD_DIM = 64
STATE = 64
DI = 2048


def from_behind(value, axis, steps):
    count = lax.axis_size(axis)
    leading, last = (max(0, -steps), min(count, count - steps))
    return lax.ppermute(value, axis, [(source, source + steps) for source in range(leading, last)])


def local_scan(inner_seq, inject, readout, log_decay, step_size):
    signal = inner_seq.astype(jnp.float32)
    cum_decay = jnp.cumsum(log_decay, axis=0)
    scores = jnp.dot(readout, inject.T, preferred_element_type=jnp.float32)
    log_span = cum_decay[:, None, :] - cum_decay[None, :, :]
    length = log_decay.shape[0]
    causal = jnp.arange(length)[:, None] >= jnp.arange(length)[None, :]
    decay_mask = jnp.where(causal[:, :, None], jnp.exp(jnp.minimum(log_span, 0.0)), 0.0)
    weights = decay_mask * scores[:, :, None] * step_size[None, :, :]
    local_out = jnp.einsum("srh,rhp->shp", weights, signal, precision=lax.Precision.HIGHEST)
    tail_weight = jnp.exp(cum_decay[-1][None, :] - cum_decay) * step_size
    end_state = jnp.einsum(
        "rhp,rn->hpn",
        tail_weight[:, :, None] * signal,
        inject.astype(jnp.float32),
        precision=lax.Precision.HIGHEST,
    )
    return (local_out, end_state, cum_decay[-1], cum_decay)


def apply_start(local_out, cum_decay, readout, inner_seq, skip_gain, start_state):
    carried = jnp.einsum(
        "sn,hpn->shp", readout.astype(jnp.float32), start_state, precision=lax.Precision.HIGHEST
    )
    return (
        local_out
        + jnp.exp(cum_decay)[:, :, None] * carried
        + skip_gain[None, :, None] * inner_seq.astype(jnp.float32)
    )


def space_carry(end_state, total_decay):
    growth = jnp.exp(total_decay)[..., None, None]

    def relay_step(loop_index, start_state):
        return from_behind(growth * start_state + end_state, "space", 1)

    return lax.fori_loop(0, lax.axis_size("space") - 1, relay_step, jnp.zeros_like(end_state))


def body(
    tokens,
    w_in,
    w_out,
    a_log_time,
    a_log_space,
    dt_bias_time,
    dt_bias_space,
    skip_time,
    skip_space,
    norm_gain,
):
    base = 2 * DI
    w_time = jnp.concatenate(
        [
            w_in[:, DI:base],
            w_in[:, base : base + 2 * STATE],
            w_in[:, base + 4 * STATE : base + 4 * STATE + HEADS],
        ],
        axis=1,
    )
    w_home = jnp.concatenate(
        [
            w_in[:, :DI],
            w_in[:, base + 2 * STATE : base + 4 * STATE],
            w_in[:, base + 4 * STATE + HEADS :],
        ],
        axis=1,
    )
    fr_dev, rows_dev, cols_dev = (tokens.shape[0], tokens.shape[1], tokens.shape[2])
    n_tm = lax.axis_size("tm")
    flat_tokens = tokens.reshape(-1, D)
    home = jnp.dot(flat_tokens, w_home, preferred_element_type=jnp.float32)
    gate_z = home[:, :DI].astype(jnp.bfloat16)
    b_space = home[:, DI : DI + STATE].astype(jnp.bfloat16)
    c_space = home[:, DI + STATE : DI + 2 * STATE].astype(jnp.bfloat16)
    step_space = jax.nn.softplus(home[:, DI + 2 * STATE :] + dt_bias_space)
    decay_space = -jnp.exp(a_log_space) * step_space
    scan_all = jax.vmap(local_scan)
    time_pack = jnp.dot(flat_tokens, w_time, preferred_element_type=jnp.float32).astype(
        jnp.bfloat16
    )
    sending = time_pack.reshape(fr_dev, n_tm, -1, time_pack.shape[-1])
    time_pack = lax.all_to_all(sending, "tm", split_axis=1, concat_axis=0, tiled=True)
    frames = time_pack.shape[0]
    item_count = time_pack.shape[2]
    sequences = jnp.swapaxes(time_pack[:, 0], 0, 1)
    inner_seq = sequences[..., :DI].reshape(item_count, frames, HEADS, HEAD_DIM)
    inject = sequences[..., DI : DI + STATE]
    readout = sequences[..., DI + STATE : DI + 2 * STATE]
    raw_step = sequences[..., DI + 2 * STATE :].astype(jnp.float32)
    step_size = jax.nn.softplus(raw_step + dt_bias_time)
    log_decay = -jnp.exp(a_log_time) * step_size
    time_local_out, unused_end, unused_total, unused_cum = scan_all(
        inner_seq, inject, readout, log_decay, step_size
    )
    result = time_local_out + skip_time[None, None, :, None] * inner_seq.astype(jnp.float32)
    result = result.astype(jnp.bfloat16).reshape(item_count, frames, DI)
    returned = jnp.swapaxes(result, 0, 1)[:, None]
    time_out = lax.all_to_all(returned, "tm", split_axis=0, concat_axis=1, tiled=True)
    space_in = time_out.reshape(fr_dev, rows_dev, cols_dev, HEADS, HEAD_DIM)
    inject_grid = b_space.reshape(fr_dev, rows_dev, cols_dev, STATE)
    readout_grid = c_space.reshape(fr_dev, rows_dev, cols_dev, STATE)
    decay_grid = decay_space.reshape(fr_dev, rows_dev, cols_dev, HEADS)
    step_grid = step_space.reshape(fr_dev, rows_dev, cols_dev, HEADS)
    apply_all = jax.vmap(apply_start, in_axes=(0, 0, 0, 0, None, 0))
    state_now = jnp.zeros((fr_dev, HEADS, HEAD_DIM, STATE), jnp.float32)
    decay_sum = jnp.zeros((fr_dev, HEADS), jnp.float32)
    row_results = []
    row_offsets = []
    for row_index in range(rows_dev):
        inner_row = space_in[:, row_index]
        readout_row = readout_grid[:, row_index]
        local_out, end_state, total_decay, cum_decay = scan_all(
            inner_row,
            inject_grid[:, row_index],
            readout_row,
            decay_grid[:, row_index],
            step_grid[:, row_index],
        )
        row_results.append(
            apply_all(local_out, cum_decay, readout_row, inner_row, skip_space, state_now)
        )
        row_offsets.append(cum_decay + decay_sum[:, None, :])
        state_now = jnp.exp(total_decay)[..., None, None] * state_now + end_state
        decay_sum = decay_sum + total_decay
    space_start = space_carry(state_now, decay_sum)
    finished = []
    for row_index in range(rows_dev):
        carried = jnp.einsum(
            "fsn,fhpn->fshp",
            readout_grid[:, row_index].astype(jnp.float32),
            space_start,
            precision=lax.Precision.HIGHEST,
        )
        finished.append(
            row_results[row_index] + jnp.exp(row_offsets[row_index])[..., None] * carried
        )
    space_out = jnp.stack(finished, axis=1).reshape(-1, DI)
    gated = space_out * jax.nn.silu(gate_z.astype(jnp.float32))
    inv_scale = lax.rsqrt(jnp.mean(gated * gated, axis=-1, keepdims=True) + 1e-05)
    normed = (gated * inv_scale * norm_gain).astype(jnp.bfloat16)
    summed = jnp.dot(normed, w_out, preferred_element_type=jnp.float32) + flat_tokens.astype(
        jnp.float32
    )
    return summed.astype(jnp.bfloat16).reshape(tokens.shape)


def solution(mesh):
    placed = (P("tm", "space", None, None), P(), P(), P(), P(), P(), P(), P(), P(), P())
    return jax.shard_map(
        body, mesh=mesh, in_specs=placed, out_specs=P("tm", "space", None, None), check_vma=False
    )
```

profile of v0, /device:TPU:22, one launch (start us, length us, event | category | flops | bytes accessed | tf_op | source)
XLA Modules:
  0.0 1088.4 jit_solution(10576895644700840184)
XLA Ops:
  3.8 6.4 fusion.41
  10.2 7.3 reshape.156
  17.5 8.0 copy.171
  25.5 8.5 all-to-all-start
  38.7 53.3 %all-to-all-done = bf16[4,16,15,2208]{3,0,2,1:T(4,128)(2,1)} async-done(((bf16[4,16,15,2208]{3,0,2,1:T(4,128)(2,1)}), bf16[4,16,15,2208]{3,0,2,1:T(4,128)(2,1)}, u32[]{:S(2)}, u32[]{:S(2)}) %all-to-all-start) | async-done | bytes 4239392 | tf_op jit(solution)/shard_map/all_to_all | solution.py:102
  92.0 6.4 copy.172
  98.4 7.5 squeeze.58
  105.9 9.3 copy.173
  115.2 7.0 slice.135
  125.0 6.3 fusion.153
  131.6 20.5 %fusion = bf16[15,64,32,64]{1,3,2,0:T(8,128)(2,1)} fusion(bf16[15,64,32,64]{1,3,2,0:T(8,128)(2,1)} %bitcast.194, f32[32]{0:T(128)S(1)} %copy-done.25, f32[15,64,32]{1,2,0:T(8,128)S(1)} %get-tuple-element.43, f32[15,64,64]{2,1,0:T(8,128)S(1)} %fusion.101, f32[15,64,32]{1,2,0:T(8,128)S(1)} %copy.175, pred[64,64]{1,0:T(8,128)(4,1)S(1)} %iota_compare_fusion.1), kind=kOutput, calls=%fused_computation.2 | convolution fusion | flops 1527644160 | bytes 8360064 | tf_op jit(solution)/shard_map/vmap(srh,rhp->shp)/dot_general | solution.py:28
  152.1 10.0 copy.179
  162.1 7.9 all-to-all-start.1
  170.1 9.6 fusion.152
  192.1 32.8 %all-to-all-done.1 = bf16[64,1,15,2048]{3,2,1,0:T(8,128)(2,1)} async-done(((bf16[64,1,15,2048]{3,2,1,0:T(8,128)(2,1)}), bf16[64,1,15,2048]{3,2,1,0:T(8,128)(2,1)}, u32[]{:S(2)}, u32[]{:S(2)}) %all-to-all-start.1) | async-done | bytes 3932192 | tf_op jit(solution)/shard_map/all_to_all | solution.py:118
  234.1 23.2 %reshape.159 = bf16[4,3,80,32,64]{4,3,0,2,1:T(8,128)(2,1)} reshape(bf16[4,16,1,15,2048]{4,0,3,1,2:T(4,128)(2,1)} %copy.181) | data formatting | bytes 7864320 | tf_op jit(solution)/shard_map/reshape | solution.py:119
  257.3 6.1 fusion.149
  297.0 693.8 %while.10 = (s32[]{:T(128)}, f32[4,32,64,64]{3,2,1,0:T(8,128)}, f32[4,32,1,1]{1,0,3,2:T(4,128)S(1)}, f32[4,32,64,64]{3,2,1,0:T(8,128)}, s32[]{:T(128)}) while((s32[]{:T(128)}, f32[4,32,64,64]{3,2,1,0:T(8,128)}, f32[4,32,1,1]{1,0,3,2:T(4,128)S(1)}, f32[4,32,64,64]{3,2,1,0:T(8,128)}, s32[]{:T(128)}) %tuple.48), condition=%wide.region_5.6_spmd, body=%wide.region_4.5_spmd.sunk | while | flops 1048578 | bytes 14680677 | solution.py:56
  305.8 93.0 %collective-permute-done = f32[4,32,64,64]{3,2,1,0:T(8,128)} collective-permute-done((f32[4,32,64,64]{3,2,1,0:T(8,128)}, f32[4,32,64,64]{3,2,1,0:T(8,128)}, u32[]{:S(2)}, u32[]{:S(2)}) %collective-permute-start) | collective-permute-done | bytes 2097184 | tf_op jit(solution)/shard_map/while/body/eval_jaxpr/ppermute | solution.py:16
  406.7 93.0 %collective-permute-done = f32[4,32,64,64]{3,2,1,0:T(8,128)} collective-permute-done((f32[4,32,64,64]{3,2,1,0:T(8,128)}, f32[4,32,64,64]{3,2,1,0:T(8,128)}, u32[]{:S(2)}, u32[]{:S(2)}) %collective-permute-start) | collective-permute-done | bytes 2097184 | tf_op jit(solution)/shard_map/while/body/eval_jaxpr/ppermute | solution.py:16
  507.5 92.2 %collective-permute-done = f32[4,32,64,64]{3,2,1,0:T(8,128)} collective-permute-done((f32[4,32,64,64]{3,2,1,0:T(8,128)}, f32[4,32,64,64]{3,2,1,0:T(8,128)}, u32[]{:S(2)}, u32[]{:S(2)}) %collective-permute-start) | collective-permute-done | bytes 2097184 | tf_op jit(solution)/shard_map/while/body/eval_jaxpr/ppermute | solution.py:16
  607.6 91.3 %collective-permute-done = f32[4,32,64,64]{3,2,1,0:T(8,128)} collective-permute-done((f32[4,32,64,64]{3,2,1,0:T(8,128)}, f32[4,32,64,64]{3,2,1,0:T(8,128)}, u32[]{:S(2)}, u32[]{:S(2)}) %collective-permute-start) | collective-permute-done | bytes 2097184 | tf_op jit(solution)/shard_map/while/body/eval_jaxpr/ppermute | solution.py:16
  706.7 90.4 %collective-permute-done = f32[4,32,64,64]{3,2,1,0:T(8,128)} collective-permute-done((f32[4,32,64,64]{3,2,1,0:T(8,128)}, f32[4,32,64,64]{3,2,1,0:T(8,128)}, u32[]{:S(2)}, u32[]{:S(2)}) %collective-permute-start) | collective-permute-done | bytes 2097184 | tf_op jit(solution)/shard_map/while/body/eval_jaxpr/ppermute | solution.py:16
  804.9 89.5 %collective-permute-done = f32[4,32,64,64]{3,2,1,0:T(8,128)} collective-permute-done((f32[4,32,64,64]{3,2,1,0:T(8,128)}, f32[4,32,64,64]{3,2,1,0:T(8,128)}, u32[]{:S(2)}, u32[]{:S(2)}) %collective-permute-start) | collective-permute-done | bytes 2097184 | tf_op jit(solution)/shard_map/while/body/eval_jaxpr/ppermute | solution.py:16
  902.2 88.5 %collective-permute-done = f32[4,32,64,64]{3,2,1,0:T(8,128)} collective-permute-done((f32[4,32,64,64]{3,2,1,0:T(8,128)}, f32[4,32,64,64]{3,2,1,0:T(8,128)}, u32[]{:S(2)}, u32[]{:S(2)}) %collective-permute-start) | collective-permute-done | bytes 2097184 | tf_op jit(solution)/shard_map/while/body/eval_jaxpr/ppermute | solution.py:16
  1004.6 7.6 fusion.52
  1012.4 7.8 fusion.57
  1020.2 8.1 fusion.61
  1028.4 10.6 pad_maximum_fusion
  1039.0 18.0 %copy.214 = f32[4,3,80,32,64]{4,3,2,1,0:T(8,128)} copy(f32[4,3,80,32,64]{2,4,3,0,1:T(8,128)} %pad_maximum_fusion) | data formatting | bytes 15728640 | tf_op jit(solution)/shard_map/stack | solution.py:157
  1056.9 14.5 %reshape.164 = f32[960,2048]{1,0:T(8,128)} reshape(f32[4,3,80,32,64]{4,3,2,1,0:T(8,128)} %copy.214) | data formatting | bytes 15728640 | tf_op jit(solution)/shard_map/reshape | solution.py:157
  1078.6 9.3 add_convert_fusion
  (126 shorter events, 143.3 us)
Async XLA Ops:
  25.5 66.4 %all-to-all-start = ((bf16[4,16,15,2208]{3,0,2,1:T(4,128)(2,1)}), bf16[4,16,15,2208]{3,0,2,1:T(4,128)(2,1)}, u32[]{:S(2)}, u32[]{:S(2)}) async-start(bf16[4,16,15,2208]{3,0,2,1:T(4,128)(2,1)} %copy.171), calls=%async_computation | async-start | bytes 8847360 | tf_op jit(solution)/shard_map/all_to_all | solution.py:102
  34.0 4.6 copy-start.23
  34.0 4.6 copy-start.24
  115.2 8.4 copy-start.19
  115.2 16.4 %copy-start.25 = (f32[32]{0:T(128)S(1)}, f32[32]{0:T(128)}, u32[]{:S(2)}) copy-start(f32[32]{0:T(128)} %param.19) | copy-start | bytes 388
  162.1 7.9 slice-start.1
  162.1 62.8 %all-to-all-start.1 = ((bf16[64,1,15,2048]{3,2,1,0:T(8,128)(2,1)}), bf16[64,1,15,2048]{3,2,1,0:T(8,128)(2,1)}, u32[]{:S(2)}, u32[]{:S(2)}) async-start(bf16[64,1,15,2048]{3,2,1,0:T(8,128)(2,1)} %bitcast.192), calls=%async_computation.1 | async-start | bytes 8388608 | tf_op jit(solution)/shard_map/all_to_all | solution.py:118
  170.1 9.6 copy-start.18
  302.9 95.9 %collective-permute-start = (f32[4,32,64,64]{3,2,1,0:T(8,128)}, f32[4,32,64,64]{3,2,1,0:T(8,128)}, u32[]{:S(2)}, u32[]{:S(2)}) collective-permute-start(f32[4,32,64,64]{3,2,1,0:T(8,128)} %multiply_add_fusion.4), channel_id=1, source_target_pairs={{0,1},{1,2},{2,3},{3,4},{4,5},{5,6},{6,7},{8,9},{9,10},{10,11},{11... | collective-permute-start | bytes 6291464 | tf_op jit(solution)/shard_map/while/body/eval_jaxpr/ppermute | solution.py:16
  404.6 95.1 %collective-permute-start = (f32[4,32,64,64]{3,2,1,0:T(8,128)}, f32[4,32,64,64]{3,2,1,0:T(8,128)}, u32[]{:S(2)}, u32[]{:S(2)}) collective-permute-start(f32[4,32,64,64]{3,2,1,0:T(8,128)} %multiply_add_fusion.4), channel_id=1, source_target_pairs={{0,1},{1,2},{2,3},{3,4},{4,5},{5,6},{6,7},{8,9},{9,10},{10,11},{11... | collective-permute-start | bytes 6291464 | tf_op jit(solution)/shard_map/while/body/eval_jaxpr/ppermute | solution.py:16
  505.6 94.1 %collective-permute-start = (f32[4,32,64,64]{3,2,1,0:T(8,128)}, f32[4,32,64,64]{3,2,1,0:T(8,128)}, u32[]{:S(2)}, u32[]{:S(2)}) collective-permute-start(f32[4,32,64,64]{3,2,1,0:T(8,128)} %multiply_add_fusion.4), channel_id=1, source_target_pairs={{0,1},{1,2},{2,3},{3,4},{4,5},{5,6},{6,7},{8,9},{9,10},{10,11},{11... | collective-permute-start | bytes 6291464 | tf_op jit(solution)/shard_map/while/body/eval_jaxpr/ppermute | solution.py:16
  605.7 93.2 %collective-permute-start = (f32[4,32,64,64]{3,2,1,0:T(8,128)}, f32[4,32,64,64]{3,2,1,0:T(8,128)}, u32[]{:S(2)}, u32[]{:S(2)}) collective-permute-start(f32[4,32,64,64]{3,2,1,0:T(8,128)} %multiply_add_fusion.4), channel_id=1, source_target_pairs={{0,1},{1,2},{2,3},{3,4},{4,5},{5,6},{6,7},{8,9},{9,10},{10,11},{11... | collective-permute-start | bytes 6291464 | tf_op jit(solution)/shard_map/while/body/eval_jaxpr/ppermute | solution.py:16
  704.8 92.3 %collective-permute-start = (f32[4,32,64,64]{3,2,1,0:T(8,128)}, f32[4,32,64,64]{3,2,1,0:T(8,128)}, u32[]{:S(2)}, u32[]{:S(2)}) collective-permute-start(f32[4,32,64,64]{3,2,1,0:T(8,128)} %multiply_add_fusion.4), channel_id=1, source_target_pairs={{0,1},{1,2},{2,3},{3,4},{4,5},{5,6},{6,7},{8,9},{9,10},{10,11},{11... | collective-permute-start | bytes 6291464 | tf_op jit(solution)/shard_map/while/body/eval_jaxpr/ppermute | solution.py:16
  803.0 91.4 %collective-permute-start = (f32[4,32,64,64]{3,2,1,0:T(8,128)}, f32[4,32,64,64]{3,2,1,0:T(8,128)}, u32[]{:S(2)}, u32[]{:S(2)}) collective-permute-start(f32[4,32,64,64]{3,2,1,0:T(8,128)} %multiply_add_fusion.4), channel_id=1, source_target_pairs={{0,1},{1,2},{2,3},{3,4},{4,5},{5,6},{6,7},{8,9},{9,10},{10,11},{11... | collective-permute-start | bytes 6291464 | tf_op jit(solution)/shard_map/while/body/eval_jaxpr/ppermute | solution.py:16
  900.3 90.5 %collective-permute-start = (f32[4,32,64,64]{3,2,1,0:T(8,128)}, f32[4,32,64,64]{3,2,1,0:T(8,128)}, u32[]{:S(2)}, u32[]{:S(2)}) collective-permute-start(f32[4,32,64,64]{3,2,1,0:T(8,128)} %multiply_add_fusion.4), channel_id=1, source_target_pairs={{0,1},{1,2},{2,3},{3,4},{4,5},{5,6},{6,7},{8,9},{9,10},{10,11},{11... | collective-permute-start | bytes 6291464 | tf_op jit(solution)/shard_map/while/body/eval_jaxpr/ppermute | solution.py:16
  994.7 4.2 copy-start.15
  999.0 5.6 copy-start.1
  999.0 5.6 copy-start.17
  1004.6 7.7 copy-start.4
  1004.6 7.7 copy-start.7
  1004.6 7.7 copy-start.11
  1004.6 7.7 copy-start.12
  1004.6 7.7 copy-start.14
  1012.3 7.9 copy-start.6
  1012.3 7.9 copy-start.8
  1012.3 7.9 copy-start.9
  1012.3 7.9 copy-start.10
  1012.4 7.9 copy-start.13
  1020.2 8.1 copy-start.2
  1071.4 6.7 copy-start
  1071.4 7.2 copy-start.21
  1071.4 7.2 copy-start.22
  (5 other events, 16.8 us)
where the time goes:
time: 1100 us; the launch traced here: 1090 us
  waiting for transfers between devices  724 us (66%)
  local copies, waits for them, and re-layouts  161 us (15%)
  matrix products  105 us (10%)
  other arithmetic  66.9 us (6%)
  starting transfers between devices  30.9 us (3%)
    ppermute x7, waiting for transfers between devices, from_behind(): lax.ppermute(value, axis, [(source, source + steps) for source in range(l...  638 us
    all_to_all x1, waiting for transfers between devices, body(): lax.all_to_all(sending, 'tm', split_axis=1, concat_axis=0, tiled=True)  53.3 us
    dot_general x4, matrix products, local_scan(): jnp.einsum('srh,rhp->shp', weights, signal, precision=lax.Precision.HIGHEST)  42.1 us
    add x7, other arithmetic, relay_step(): return from_behind(growth * start_state + end_state, 'space', 1)  41.3 us
    all_to_all x1, waiting for transfers between devices, body(): lax.all_to_all(returned, 'tm', split_axis=0, concat_axis=1, tiled=True)  32.8 us
    reshape x1, local copies, waits for them, and re-layouts, body(): space_in = time_out.reshape(fr_dev, rows_dev, cols_dev, HEADS, HEAD_DIM)  23.2 us
  transfers between devices with their start and end apart: 9, of which 9 were waited for; matrix products, arithmetic and copies ran while one was open for 2% of the time, Pallas kernels for 0%

commit v1 on v0

--- a/solution.py
+++ b/solution.py
@@ -8,6 +8,18 @@
 HEAD_DIM = 64
 STATE = 64
 DI = 2048
+
+
+def put_positions(original, peer_axis, dim_no, dim_i):
+    return jnp.concatenate(
+        lax.all_to_all(
+            jnp.stack(jnp.split(original, lax.psum(1, axis_name=peer_axis), axis=dim_no)),
+            peer_axis,
+            split_axis=0,
+            concat_axis=0,
+        ),
+        axis=dim_i,
+    )
 
 
 def from_behind(value, axis, steps):
@@ -115,7 +127,7 @@
     result = time_local_out + skip_time[None, None, :, None] * inner_seq.astype(jnp.float32)
     result = result.astype(jnp.bfloat16).reshape(item_count, frames, DI)
     returned = jnp.swapaxes(result, 0, 1)[:, None]
-    time_out = lax.all_to_all(returned, "tm", split_axis=0, concat_axis=1, tiled=True)
+    time_out = put_positions(returned, "tm", 0, 1)
     space_in = time_out.reshape(fr_dev, rows_dev, cols_dev, HEADS, HEAD_DIM)
     inject_grid = b_space.reshape(fr_dev, rows_dev, cols_dev, STATE)
     readout_grid = c_space.reshape(fr_dev, rows_dev, cols_dev, STATE)

time: 1100 us -> 1100 us (level)
    unnamed x55 -> x72, local copies, waits for them, and re-layouts: 16.8 us -> 44.6 us
    reshape x1 -> x0, local copies, waits for them, and re-layouts: 23.2 us -> none  [body(): space_in = time_out.reshape(fr_dev, rows_dev, cols_dev, HEADS, HEAD_DIM)]
    another operation x1 -> x3, local copies, waits for them, and re-layouts: 2.55 us -> 16.6 us  [the longest x1 12.2 us: body(): space_in = time_out.reshape(fr_dev, rows_dev, cols_dev, HEADS, HEAD_DIM)]
where the time goes in v1:
time: 1100 us; the launch traced here: 1090 us
  waiting for transfers between devices  720 us (65%)
  local copies, waits for them, and re-layouts  169 us (15%)
  matrix products  104 us (9%)
  other arithmetic  66.9 us (6%)
  starting transfers between devices  30.8 us (3%)
    ppermute x7, waiting for transfers between devices, from_behind(): lax.ppermute(value, axis, [(source, source + steps) for source in range(l...  638 us
    all_to_all x1, waiting for transfers between devices, body(): lax.all_to_all(sending, 'tm', split_axis=1, concat_axis=0, tiled=True)  53.3 us
    unnamed x72, local copies, waits for them, and re-layouts  44.6 us
    dot_general x4, matrix products, local_scan(): jnp.einsum('srh,rhp->shp', weights, signal, precision=lax.Precision.HIGHEST)  42.1 us
    add x7, other arithmetic, relay_step(): return from_behind(growth * start_state + end_state, 'space', 1)  41.3 us
    all_to_all x1, waiting for transfers between devices, put_positions(): lax.all_to_all(jnp.stack(jnp.split(original, lax.psum(1, axis_name=peer_a...  29.2 us
  transfers between devices with their start and end apart: 9, of which 9 were waited for; matrix products, arithmetic and copies ran while one was open for 2% of the time, Pallas kernels for 0%

profile of v1, /device:TPU:22, one launch (start us, length us, event | category | flops | bytes accessed | tf_op | source)
XLA Modules:
  0.0 1091.7 jit_solution(16451995118966513586)
XLA Ops:
  3.8 6.4 fusion.41
  10.2 7.3 reshape.187
  17.5 8.0 copy.197
  25.5 8.5 all-to-all-start
  38.7 53.3 %all-to-all-done = bf16[4,16,15,2208]{3,0,2,1:T(4,128)(2,1)} async-done(((bf16[4,16,15,2208]{3,0,2,1:T(4,128)(2,1)}), bf16[4,16,15,2208]{3,0,2,1:T(4,128)(2,1)}, u32[]{:S(2)}, u32[]{:S(2)}) %all-to-all-start) | async-done | bytes 4239392 | tf_op jit(solution)/shard_map/all_to_all | solution.py:114
  92.0 6.4 copy.198
  98.3 7.5 squeeze.58
  105.8 9.4 copy.199
  115.2 7.0 slice.151
  125.0 6.3 fusion.169
  131.6 20.5 %fusion = bf16[15,64,32,64]{1,3,2,0:T(8,128)(2,1)} fusion(bf16[15,64,32,64]{1,3,2,0:T(8,128)(2,1)} %bitcast.267, f32[32]{0:T(128)S(1)} %copy-done.26, f32[15,64,32]{1,2,0:T(8,128)S(1)} %get-tuple-element.43, f32[15,64,64]{2,1,0:T(8,128)S(1)} %fusion.117, f32[15,64,32]{1,2,0:T(8,128)S(1)} %copy.201, pred[64,64]{1,0:T(8,128)(4,1)S(1)} %iota_compare_fusion.1), kind=kOutput, calls=%fused_computation.2 | convolution fusion | flops 1527644160 | bytes 8360064 | tf_op jit(solution)/shard_map/vmap(srh,rhp->shp)/dot_general | solution.py:40
  152.1 8.4 copy.205
  190.2 7.9 all-to-all-start.1
  198.1 9.6 fusion.168
  220.2 29.2 %all-to-all-done.1 = bf16[16,4,1,15,2048]{4,1,3,2,0:T(4,128)(2,1)} async-done(((bf16[16,4,1,15,2048]{4,1,3,2,0:T(4,128)(2,1)}), bf16[16,4,1,15,2048]{4,1,3,2,0:T(4,128)(2,1)}, u32[]{:S(2)}, u32[]{:S(2)}) %all-to-all-start.1) | async-done | bytes 3932192 | tf_op jit(solution)/shard_map/all_to_all | solution.py:15
  249.4 12.2 %reshape_reshape.3 = bf16[4,3,80,32,64]{4,3,0,2,1:T(8,128)(2,1)} reshape(bf16[4,16,1,15,2048]{4,0,3,2,1:T(4,128)(2,1)} %bitcast.26) | data formatting | bytes 7864320 | tf_op jit(solution)/shard_map/reshape;reshape | solution.py:131
  261.6 6.1 fusion.165
  297.6 693.8 %while.10 = (s32[]{:T(128)}, f32[4,32,64,64]{3,2,1,0:T(8,128)}, f32[4,32,1,1]{1,0,3,2:T(4,128)S(1)}, f32[4,32,64,64]{3,2,1,0:T(8,128)}, s32[]{:T(128)}) while((s32[]{:T(128)}, f32[4,32,64,64]{3,2,1,0:T(8,128)}, f32[4,32,1,1]{1,0,3,2:T(4,128)S(1)}, f32[4,32,64,64]{3,2,1,0:T(8,128)}, s32[]{:T(128)}) %tuple.48), condition=%wide.region_5.6_spmd, body=%wide.region_4.5_spmd.sunk | while | flops 1048578 | bytes 14680677 | solution.py:68
  306.4 92.9 %collective-permute-done = f32[4,32,64,64]{3,2,1,0:T(8,128)} collective-permute-done((f32[4,32,64,64]{3,2,1,0:T(8,128)}, f32[4,32,64,64]{3,2,1,0:T(8,128)}, u32[]{:S(2)}, u32[]{:S(2)}) %collective-permute-start) | collective-permute-done | bytes 2097184 | tf_op jit(solution)/shard_map/while/body/eval_jaxpr/ppermute | solution.py:28
  407.3 93.0 %collective-permute-done = f32[4,32,64,64]{3,2,1,0:T(8,128)} collective-permute-done((f32[4,32,64,64]{3,2,1,0:T(8,128)}, f32[4,32,64,64]{3,2,1,0:T(8,128)}, u32[]{:S(2)}, u32[]{:S(2)}) %collective-permute-start) | collective-permute-done | bytes 2097184 | tf_op jit(solution)/shard_map/while/body/eval_jaxpr/ppermute | solution.py:28
  508.2 92.2 %collective-permute-done = f32[4,32,64,64]{3,2,1,0:T(8,128)} collective-permute-done((f32[4,32,64,64]{3,2,1,0:T(8,128)}, f32[4,32,64,64]{3,2,1,0:T(8,128)}, u32[]{:S(2)}, u32[]{:S(2)}) %collective-permute-start) | collective-permute-done | bytes 2097184 | tf_op jit(solution)/shard_map/while/body/eval_jaxpr/ppermute | solution.py:28
  608.2 91.3 %collective-permute-done = f32[4,32,64,64]{3,2,1,0:T(8,128)} collective-permute-done((f32[4,32,64,64]{3,2,1,0:T(8,128)}, f32[4,32,64,64]{3,2,1,0:T(8,128)}, u32[]{:S(2)}, u32[]{:S(2)}) %collective-permute-start) | collective-permute-done | bytes 2097184 | tf_op jit(solution)/shard_map/while/body/eval_jaxpr/ppermute | solution.py:28
  707.3 90.4 %collective-permute-done = f32[4,32,64,64]{3,2,1,0:T(8,128)} collective-permute-done((f32[4,32,64,64]{3,2,1,0:T(8,128)}, f32[4,32,64,64]{3,2,1,0:T(8,128)}, u32[]{:S(2)}, u32[]{:S(2)}) %collective-permute-start) | collective-permute-done | bytes 2097184 | tf_op jit(solution)/shard_map/while/body/eval_jaxpr/ppermute | solution.py:28
  805.5 89.5 %collective-permute-done = f32[4,32,64,64]{3,2,1,0:T(8,128)} collective-permute-done((f32[4,32,64,64]{3,2,1,0:T(8,128)}, f32[4,32,64,64]{3,2,1,0:T(8,128)}, u32[]{:S(2)}, u32[]{:S(2)}) %collective-permute-start) | collective-permute-done | bytes 2097184 | tf_op jit(solution)/shard_map/while/body/eval_jaxpr/ppermute | solution.py:28
  902.8 88.5 %collective-permute-done = f32[4,32,64,64]{3,2,1,0:T(8,128)} collective-permute-done((f32[4,32,64,64]{3,2,1,0:T(8,128)}, f32[4,32,64,64]{3,2,1,0:T(8,128)}, u32[]{:S(2)}, u32[]{:S(2)}) %collective-permute-start) | collective-permute-done | bytes 2097184 | tf_op jit(solution)/shard_map/while/body/eval_jaxpr/ppermute | solution.py:28
  1008.0 7.6 fusion.52
  1015.7 8.1 fusion.61
  1023.8 7.9 fusion.57
  1031.7 10.6 pad_maximum_fusion
  1042.3 17.9 %copy.238 = f32[4,3,80,32,64]{4,3,2,1,0:T(8,128)} copy(f32[4,3,80,32,64]{2,4,3,0,1:T(8,128)} %pad_maximum_fusion) | data formatting | bytes 15728640 | tf_op jit(solution)/shard_map/stack | solution.py:169
  1060.2 14.5 %reshape.195 = f32[960,2048]{1,0:T(8,128)} reshape(f32[4,3,80,32,64]{4,3,2,1,0:T(8,128)} %copy.238) | data formatting | bytes 15728640 | tf_op jit(solution)/shard_map/reshape | solution.py:169
  1081.9 9.3 add_convert_fusion
  (142 shorter events, 162.7 us)
Async XLA Ops:
  25.5 66.4 %all-to-all-start = ((bf16[4,16,15,2208]{3,0,2,1:T(4,128)(2,1)}), bf16[4,16,15,2208]{3,0,2,1:T(4,128)(2,1)}, u32[]{:S(2)}, u32[]{:S(2)}) async-start(bf16[4,16,15,2208]{3,0,2,1:T(4,128)(2,1)} %copy.197), calls=%async_computation | async-start | bytes 8847360 | tf_op jit(solution)/shard_map/all_to_all | solution.py:114
  34.0 4.6 copy-start.24
  34.0 4.6 copy-start.25
  115.2 8.4 copy-start.20
  115.2 16.4 %copy-start.26 = (f32[32]{0:T(128)S(1)}, f32[32]{0:T(128)}, u32[]{:S(2)}) copy-start(f32[32]{0:T(128)} %param.19) | copy-start | bytes 388
  188.3 9.8 slice-start.1
  190.2 59.2 %all-to-all-start.1 = ((bf16[16,4,1,15,2048]{4,1,3,2,0:T(4,128)(2,1)}), bf16[16,4,1,15,2048]{4,1,3,2,0:T(4,128)(2,1)}, u32[]{:S(2)}, u32[]{:S(2)}) async-start(bf16[16,4,1,15,2048]{4,1,3,2,0:T(4,128)(2,1)} %fusion.101), calls=%async_computation.1 | async-start | bytes 7864320 | tf_op jit(solution)/shard_map/all_to_all | solution.py:15
  198.1 9.6 copy-start.19
  287.6 3.6 copy-start.7
  303.5 95.9 %collective-permute-start = (f32[4,32,64,64]{3,2,1,0:T(8,128)}, f32[4,32,64,64]{3,2,1,0:T(8,128)}, u32[]{:S(2)}, u32[]{:S(2)}) collective-permute-start(f32[4,32,64,64]{3,2,1,0:T(8,128)} %multiply_add_fusion.4), channel_id=1, source_target_pairs={{0,1},{1,2},{2,3},{3,4},{4,5},{5,6},{6,7},{8,9},{9,10},{10,11},{11... | collective-permute-start | bytes 6291464 | tf_op jit(solution)/shard_map/while/body/eval_jaxpr/ppermute | solution.py:28
  405.3 95.1 %collective-permute-start = (f32[4,32,64,64]{3,2,1,0:T(8,128)}, f32[4,32,64,64]{3,2,1,0:T(8,128)}, u32[]{:S(2)}, u32[]{:S(2)}) collective-permute-start(f32[4,32,64,64]{3,2,1,0:T(8,128)} %multiply_add_fusion.4), channel_id=1, source_target_pairs={{0,1},{1,2},{2,3},{3,4},{4,5},{5,6},{6,7},{8,9},{9,10},{10,11},{11... | collective-permute-start | bytes 6291464 | tf_op jit(solution)/shard_map/while/body/eval_jaxpr/ppermute | solution.py:28
  506.2 94.1 %collective-permute-start = (f32[4,32,64,64]{3,2,1,0:T(8,128)}, f32[4,32,64,64]{3,2,1,0:T(8,128)}, u32[]{:S(2)}, u32[]{:S(2)}) collective-permute-start(f32[4,32,64,64]{3,2,1,0:T(8,128)} %multiply_add_fusion.4), channel_id=1, source_target_pairs={{0,1},{1,2},{2,3},{3,4},{4,5},{5,6},{6,7},{8,9},{9,10},{10,11},{11... | collective-permute-start | bytes 6291464 | tf_op jit(solution)/shard_map/while/body/eval_jaxpr/ppermute | solution.py:28
  606.3 93.2 %collective-permute-start = (f32[4,32,64,64]{3,2,1,0:T(8,128)}, f32[4,32,64,64]{3,2,1,0:T(8,128)}, u32[]{:S(2)}, u32[]{:S(2)}) collective-permute-start(f32[4,32,64,64]{3,2,1,0:T(8,128)} %multiply_add_fusion.4), channel_id=1, source_target_pairs={{0,1},{1,2},{2,3},{3,4},{4,5},{5,6},{6,7},{8,9},{9,10},{10,11},{11... | collective-permute-start | bytes 6291464 | tf_op jit(solution)/shard_map/while/body/eval_jaxpr/ppermute | solution.py:28
  705.4 92.3 %collective-permute-start = (f32[4,32,64,64]{3,2,1,0:T(8,128)}, f32[4,32,64,64]{3,2,1,0:T(8,128)}, u32[]{:S(2)}, u32[]{:S(2)}) collective-permute-start(f32[4,32,64,64]{3,2,1,0:T(8,128)} %multiply_add_fusion.4), channel_id=1, source_target_pairs={{0,1},{1,2},{2,3},{3,4},{4,5},{5,6},{6,7},{8,9},{9,10},{10,11},{11... | collective-permute-start | bytes 6291464 | tf_op jit(solution)/shard_map/while/body/eval_jaxpr/ppermute | solution.py:28
  803.6 91.4 %collective-permute-start = (f32[4,32,64,64]{3,2,1,0:T(8,128)}, f32[4,32,64,64]{3,2,1,0:T(8,128)}, u32[]{:S(2)}, u32[]{:S(2)}) collective-permute-start(f32[4,32,64,64]{3,2,1,0:T(8,128)} %multiply_add_fusion.4), channel_id=1, source_target_pairs={{0,1},{1,2},{2,3},{3,4},{4,5},{5,6},{6,7},{8,9},{9,10},{10,11},{11... | collective-permute-start | bytes 6291464 | tf_op jit(solution)/shard_map/while/body/eval_jaxpr/ppermute | solution.py:28
  900.9 90.5 %collective-permute-start = (f32[4,32,64,64]{3,2,1,0:T(8,128)}, f32[4,32,64,64]{3,2,1,0:T(8,128)}, u32[]{:S(2)}, u32[]{:S(2)}) collective-permute-start(f32[4,32,64,64]{3,2,1,0:T(8,128)} %multiply_add_fusion.4), channel_id=1, source_target_pairs={{0,1},{1,2},{2,3},{3,4},{4,5},{5,6},{6,7},{8,9},{9,10},{10,11},{11... | collective-permute-start | bytes 6291464 | tf_op jit(solution)/shard_map/while/body/eval_jaxpr/ppermute | solution.py:28
  995.3 4.4 copy-start.1
  1002.3 5.6 copy-start.3
  1002.3 5.6 copy-start.18
  1007.9 7.7 copy-start.8
  1007.9 7.7 copy-start.9
  1007.9 7.7 copy-start.13
  1008.0 7.7 copy-start.14
  1008.0 7.7 copy-start.15
  1015.6 8.2 copy-start.6
  1015.6 8.2 copy-start.10
  1015.7 8.1 copy-start.11
  1015.7 8.1 copy-start.12
  1023.8 7.9 copy-start.4
  1074.7 6.7 copy-start.2
  1074.7 7.2 copy-start.22
  1074.7 7.2 copy-start.23
  (6 other events, 15.4 us)
